TPU v7x, 512 devices: a whole 4x8x8 slice. The times are simulated.
512 devices in a mesh: dp: 64 (over y, x, core), fsdp: 8 (over z).
Axes of the slice: x: 4, y: 8, z: 8, core: 2. Of those that a mesh axis runs over, the one named last changes fastest.
Arguments:
- query_emb: bfloat16 [32768, 4096], P('dp', 'fsdp')
- passage_emb: bfloat16 [65536, 4096], P('dp', 'fsdp')
- cand_blocks: int32 [256, 4], P('dp'), may hold values from 0 to 511, as said below
- positive: int32 [32768], P('dp'), may hold values from 0 to 511
Outputs:
- losses: float32 [32768], P(('dp', 'fsdp'))
- query_grad: bfloat16 [32768, 4096], P('dp', 'fsdp')
Inputs may be any that keep to these rules, and one draw needn't show every extreme that they name: `cand_blocks`: each query block lists 4 different passage blocks; block b is held by dp index b // 8. The blocks listed by the 4 query blocks of one dp index are all different, at most 1 of them are held by any one dp index, and some dp index holds exactly 1 of them. `positive`: position c names row c % 128 of the block in column c // 128 of the query's list.
All inputs are finite; a program needn't handle non-finite values.
Results may differ from a plain program's by a relative error of at most 0.0038.
Values may be sent and summed in bfloat16 or wider, within the bound.
A program may use at most 64 MiB of HBM per device.

v0:
```python
import jax
import jax.numpy as jnp
from jax import lax
from jax.sharding import PartitionSpec as P


def softmax_rows(scores, positive_rows):
    row_max = jnp.max(scores, axis=1, keepdims=True)
    log_total = row_max[:, 0] + jnp.log(jnp.sum(jnp.exp(scores - row_max), axis=1))
    matched = lax.broadcasted_iota(jnp.int32, scores.shape, 1) == positive_rows[:, None]
    losses = log_total - jnp.sum(jnp.where(matched, scores, jnp.float32(0.0)), axis=1)
    weights = (jnp.exp(scores - log_total[:, None]) - matched.astype(jnp.float32)).astype(
        jnp.bfloat16
    )
    return (losses, weights)


def slot_ranks(owners):
    length = owners.shape[-1]
    same_owner = owners[..., :, None] == owners[..., None, :]
    earlier = lax.broadcasted_iota(jnp.int32, (length, length), 1) < lax.broadcasted_iota(
        jnp.int32, (length, length), 0
    )
    return jnp.sum((same_owner & earlier).astype(jnp.int32), axis=-1)


def shards(query_emb, passage_emb, cand_blocks, positive):
    dp_count = lax.axis_size("dp")
    fsdp_count = lax.axis_size("fsdp")
    query_blocks, list_len = cand_blocks.shape
    row_count, feature_count = query_emb.shape
    block_rows = row_count // query_blocks
    passage_blocks = passage_emb.shape[0] // block_rows
    capacity = (list_len * query_blocks + dp_count - 1) // dp_count
    slot_count = dp_count * capacity
    wanted = cand_blocks.reshape(-1)
    owners = wanted // passage_blocks
    local_ids = wanted % passage_blocks
    placed = owners * capacity + slot_ranks(owners)
    matched = lax.broadcasted_iota(jnp.int32, (slot_count, wanted.shape[0]), 0) == placed[None, :]
    id_table = jnp.sum(jnp.where(matched, local_ids[None, :], 0), axis=1).reshape(
        dp_count, capacity
    )
    requested = lax.all_to_all(id_table, "dp", split_axis=0, concat_axis=0, tiled=True)
    stored = passage_emb.reshape(passage_blocks, block_rows, feature_count)
    outgoing = stored[requested]
    fetched = lax.all_to_all(outgoing, "dp", split_axis=0, concat_axis=0, tiled=True)
    candidates = fetched.reshape(slot_count, block_rows, feature_count)[placed]
    candidates = candidates.reshape(query_blocks, list_len * block_rows, feature_count)
    query_rows = query_emb.reshape(query_blocks, block_rows, feature_count)
    partial_value = jnp.einsum(
        "qnd,qcd->qnc", query_rows, candidates, preferred_element_type=jnp.float32
    )
    partial_value = partial_value.reshape(row_count, list_len * block_rows)
    share_rows = row_count // fsdp_count
    first_row = lax.axis_index("fsdp") * share_rows
    scores = lax.psum(partial_value, "fsdp") * 50.0
    all_losses, weights = softmax_rows(scores, positive)
    losses = lax.dynamic_slice_in_dim(all_losses, first_row, share_rows)
    weights = weights.reshape(query_blocks, block_rows, list_len * block_rows)
    query_grad = (
        jnp.einsum("qnc,qcd->qnd", weights, candidates, preferred_element_type=jnp.float32) * 50.0
    )
    return (losses, query_grad.astype(jnp.bfloat16).reshape(row_count, feature_count))


def solution(mesh):
    return jax.shard_map(
        shards,
        mesh=mesh,
        in_specs=(P("dp", "fsdp"), P("dp", "fsdp"), P("dp", None), P("dp")),
        out_specs=(P(("dp", "fsdp")), P("dp", "fsdp")),
        check_vma=False,
    )
```

profile of v0, /device:TPU:6, one launch (start us, length us, event | category | flops | bytes accessed | tf_op | source)
XLA Modules:
  0.0 329.3 jit_solution(8835290086865391543)
XLA Ops:
  7.2 0.0 copy-start
  7.2 0.9 reshape.208
  8.0 0.2 convert_reduce_fusion
  8.2 0.1 select_reduce_fusion.1
  8.3 0.1 copy.8
  8.4 18.3 %all_to_all.14 = s32[64,1,1]{2,1,0:T(1,128)S(1)} all-to-all(s32[64,1,1]{2,1,0:T(1,128)S(1)} %copy.8), channel_id=1, replica_groups=mesh['dp'=64,'fsdp'=8] {'dp'}, dimensions={0} | all-to-all | bytes 512 | tf_op jit(solution)/shard_map/all_to_all | solution.py:44
  26.7 1.2 fusion.1
  28.0 0.0 copy-done
  28.0 5.3 %gather_fusion = bf16[64,128,512]{2,1,0:T(8,128)(2,1)} fusion(bf16[8,128,512]{2,1,0:T(8,128)(2,1)S(1)} %bitcast.21, s32[1024]{0:T(1024)S(1)} %pad_clamp_fusion.1), kind=kCustom, calls=%fused_computation | custom fusion | bytes 16777472 | tf_op jit(solution)/shard_map/gather | solution.py:46
  33.3 0.0 copy-start.3
  33.3 7.5 %all-to-all-start.1 = ((bf16[64,1,128,512]{3,2,1,0:T(8,128)(2,1)}), bf16[64,1,128,512]{3,2,1,0:T(8,128)(2,1)}, u32[]{:S(2)}, u32[]{:S(2)}) async-start(bf16[64,1,128,512]{3,2,1,0:T(8,128)(2,1)} %bitcast.22), calls=%async_computation.1 | async-start | bytes 16777216 | tf_op jit(solution)/shard_map/all_to_all | solution.py:47
  40.8 0.0 all-reduce.2.cloned.1.call-start
  40.8 0.0 copy-done.3
  40.8 0.1 reshape.210
  41.0 183.0 %all-to-all-done.1 = bf16[64,1,128,512]{3,2,1,0:T(8,128)(2,1)} async-done(((bf16[64,1,128,512]{3,2,1,0:T(8,128)(2,1)}), bf16[64,1,128,512]{3,2,1,0:T(8,128)(2,1)}, u32[]{:S(2)}, u32[]{:S(2)}) %all-to-all-start.1) | async-done | bytes 8388640 | tf_op jit(solution)/shard_map/all_to_all | solution.py:47
  223.9 4.1 %gather_fusion.1 = bf16[16,128,512]{2,1,0:T(8,128)(2,1)S(1)} fusion(bf16[64,128,512]{2,1,0:T(8,128)(2,1)} %bitcast.3, s32[1024]{0:T(1024)S(1)} %pad_clamp_fusion), kind=kCustom, calls=%fused_computation.1 | custom fusion | bytes 4194368 | tf_op jit(solution)/shard_map/gather | solution.py:48
  228.0 0.0 copy-start.2
  228.0 2.9 fusion.5
  230.9 0.0 all-reduce.2.cloned.1.call-update
  230.9 86.1 %all-reduce.2.cloned.1.call-done = f32[512,512]{1,0:T(8,128)} async-done(((f32[512,512]{1,0:T(8,128)}), f32[512,512]{1,0:T(8,128)}) %all-reduce.2.cloned.1.call-update) | async-done | bytes 1048592 | tf_op jit(solution)/shard_map/psum | solution.py:57
  317.0 0.0 copy-start.1
  317.0 1.5 multiply_reduce_fusion
  318.4 0.0 copy-done.2
  318.4 1.8 select_reduce_fusion
  320.2 0.0 copy-done.1
  320.2 0.3 subtract_convert_fusion
  320.6 1.2 fusion
  321.8 0.6 dynamic_slice.3
  (6 shorter events, 0.1 us)
Async XLA Ops:
  7.2 20.8 %copy-start = (bf16[1024,512]{1,0:T(8,128)(2,1)S(1)}, bf16[1024,512]{1,0:T(8,128)(2,1)}, u32[]{:S(2)}) copy-start(bf16[1024,512]{1,0:T(8,128)(2,1)} %param.5) | copy-start | bytes 3145732
  33.3 7.5 %copy-start.3 = (s32[4,4]{1,0:T(4,128)S(1)}, s32[4,4]{1,0:T(4,128)}, u32[]{:S(2)}) copy-start(s32[4,4]{1,0:T(4,128)} %param.6) | copy-start | bytes 196
  33.3 190.6 %all-to-all-start.1 = ((bf16[64,1,128,512]{3,2,1,0:T(8,128)(2,1)}), bf16[64,1,128,512]{3,2,1,0:T(8,128)(2,1)}, u32[]{:S(2)}, u32[]{:S(2)}) async-start(bf16[64,1,128,512]{3,2,1,0:T(8,128)(2,1)} %bitcast.22), calls=%async_computation.1 | async-start | bytes 16777216 | tf_op jit(solution)/shard_map/all_to_all | solution.py:47
  40.8 276.2 %all-reduce.2.cloned.1.call-start = ((), (), s32[]{:S(2)}) async-start(), calls=%async_computation.2 | async-start | bytes 2097152 | tf_op jit(solution)/shard_map/psum | solution.py:57
  228.0 90.4 %copy-start.2 = (s32[512]{0:T(512)S(1)}, s32[512]{0:T(512)}, u32[]{:S(2)}) copy-start(s32[512]{0:T(512)} %param.7) | copy-start | bytes 6148
  317.0 3.3 copy-start.1
Sparse Core Ops, SparseCore 0:
  231.0 85.8 all-reduce.1
where the time goes:
time: 330 us; the launch traced here: 329 us
  waiting for transfers between devices  269 us (82%)
  blocking collectives  18.3 us (6%)
  between operations  14.1 us (4%)
  local copies, waits for them, and re-layouts  11 us (3%)
  starting transfers between devices  7.51 us (2%)
  other arithmetic  5.14 us (2%)
  matrix products  4.13 us (1%)
    all_to_all x1, waiting for transfers between devices, shards(): lax.all_to_all(outgoing, 'dp', split_axis=0, concat_axis=0, tiled=True)  183 us
    psum x1, waiting for transfers between devices, shards(): scores = lax.psum(partial_value, 'fsdp') * 50.0  86.1 us
    all_to_all x1, blocking collectives, shards(): lax.all_to_all(id_table, 'dp', split_axis=0, concat_axis=0, tiled=True)  18.3 us
    all_to_all x1, starting transfers between devices, shards(): lax.all_to_all(outgoing, 'dp', split_axis=0, concat_axis=0, tiled=True)  7.47 us
  transfers between devices with their start and end apart: 2, of which 2 were waited for; matrix products, arithmetic and copies ran while one was open for 0% of the time, Pallas kernels for 0%

commit v1 on v0

--- a/solution.py
+++ b/solution.py
@@ -1,7 +1,13 @@
 import jax
 import jax.numpy as jnp
 from jax import lax
+from jax.experimental import pallas as pl
+from jax.experimental.pallas import tpu as pltpu
 from jax.sharding import PartitionSpec as P
+
+MESH = pl.DeviceIdType.MESH
+RING = 8
+ROW = 8
 
 
 def softmax_rows(scores, positive_rows):
@@ -15,37 +21,173 @@
     return (losses, weights)
 
 
-def slot_ranks(owners):
-    length = owners.shape[-1]
-    same_owner = owners[..., :, None] == owners[..., None, :]
-    earlier = lax.broadcasted_iota(jnp.int32, (length, length), 1) < lax.broadcasted_iota(
-        jnp.int32, (length, length), 0
-    )
-    return jnp.sum((same_owner & earlier).astype(jnp.int32), axis=-1)
+def fetch_kernel(
+    slots_ref, table_ref, stored_ref, out_ref,
+    r1, r2, r3, l1, l2, l3, far, stage, got, tables, table_smem,
+    ring_send, ring_recv, table_send, table_recv, slot_send, slot_recv, local_sem,
+):
+    me_dp = lax.axis_index("dp")
+    y = me_dp // ROW
+    member = me_dp % ROW
+    up = ((y + 1) % RING) * ROW + member
+    down = ((y + RING - 1) % RING) * ROW + member
+
+    def peer_of(k):
+        return (member + k) % ROW
+
+    def row_dp(k):
+        return y * ROW + peer_of(k)
+
+    barrier = pltpu.get_barrier_semaphore()
+    for target in (up, down):
+        pl.semaphore_signal(barrier, inc=1, device_id={"dp": target}, device_id_type=MESH)
+
+    def greet(k, carry):
+        pl.semaphore_signal(barrier, inc=1, device_id={"dp": row_dp(k)}, device_id_type=MESH)
+        return carry
+
+    lax.fori_loop(1, ROW, greet, 0)
+    pl.semaphore_wait(barrier, ROW + 1)
+
+    def ring_copy(index, src, dst, target):
+        return pltpu.make_async_remote_copy(
+            src_ref=src, dst_ref=dst, send_sem=ring_send.at[index], recv_sem=ring_recv.at[index],
+            device_id={"dp": target}, device_id_type=MESH,
+        )
+
+    half = stored_ref.shape[0] // 2
+    rights = [stored_ref, r1, r2, r3]
+    lefts = [stored_ref, l1, l2, l3]
+    right_copies = [ring_copy(d, rights[d], rights[d + 1], up) for d in range(3)]
+    left_copies = [ring_copy(4 + d, lefts[d], lefts[d + 1], down) for d in range(3)]
+    first, second = pl.ds(0, half), pl.ds(half, half)
+    right_copies.append(ring_copy(3, r3.at[first], far.at[first], up))
+    left_copies.append(ring_copy(7, l3.at[second], far.at[second], down))
+
+    right_copies[0].start()
+    left_copies[0].start()
+
+    def table_copy(k):
+        return pltpu.make_async_remote_copy(
+            src_ref=table_ref, dst_ref=tables.at[member],
+            send_sem=table_send.at[k], recv_sem=table_recv.at[k],
+            device_id={"dp": row_dp(k)}, device_id_type=MESH,
+        )
+
+    def start_table(k, carry):
+        table_copy(k).start()
+        return carry
+
+    def wait_table(k, carry):
+        table_copy(k).wait()
+        return carry
+
+    lax.fori_loop(1, ROW, start_table, 0)
+    own_table = pltpu.make_async_copy(table_ref, tables.at[member], local_sem.at[0])
+    own_table.start()
+    own_table.wait()
+    lax.fori_loop(1, ROW, wait_table, 0)
+    to_smem = pltpu.make_async_copy(tables, table_smem, local_sem.at[1])
+    to_smem.start()
+    to_smem.wait()
+
+    def slot_copy(delta, k):
+        return pltpu.make_async_remote_copy(
+            src_ref=stage.at[delta, k], dst_ref=got.at[delta * ROW + member],
+            send_sem=slot_send.at[delta, k], recv_sem=slot_recv.at[delta, k],
+            device_id={"dp": row_dp(k)}, device_id_type=MESH,
+        )
+
+    def serve(delta, source):
+        owner_y = (y + RING - delta) % RING
+
+        def picked(k):
+            chosen = table_smem[peer_of(k), member, owner_y]
+            return source[chosen]
+
+        def send_one(k, carry):
+            stage[delta, k] = picked(k)
+            slot_copy(delta, k).start()
+            return carry
+
+        lax.fori_loop(1, ROW, send_one, 0)
+        got[delta * ROW + member] = picked(0)
+
+    serve(0, stored_ref)
+    for d in range(1, 4):
+        right_copies[d - 1].wait_recv()
+        right_copies[d].start()
+        left_copies[d - 1].wait_recv()
+        left_copies[d].start()
+        serve(d, rights[d])
+        serve(RING - d, lefts[d])
+    right_copies[3].wait_recv()
+    left_copies[3].wait_recv()
+    serve(4, far)
+
+    def wait_slot(index, carry):
+        slot_copy(index // (ROW - 1), index % (ROW - 1) + 1).wait()
+        return carry
+
+    lax.fori_loop(0, RING * (ROW - 1), wait_slot, 0)
+    for copy in right_copies + left_copies:
+        copy.wait_send()
+
+    def place(i, carry):
+        out_ref[i] = got[slots_ref[i]]
+        return carry
+
+    lax.fori_loop(0, out_ref.shape[0], place, 0)
+
+
+def fetch(slots, table, stored):
+    block_rows, features = stored.shape[1:]
+    shard = pltpu.VMEM(stored.shape, stored.dtype)
+    vmem = pl.BlockSpec(memory_space=pltpu.VMEM)
+    return pl.pallas_call(
+        fetch_kernel,
+        out_shape=jax.ShapeDtypeStruct((slots.shape[0], block_rows, features), stored.dtype),
+        in_specs=[pl.BlockSpec(memory_space=pltpu.SMEM), vmem, vmem],
+        out_specs=vmem,
+        scratch_shapes=[shard] * 7
+        + [
+            pltpu.VMEM((RING, ROW, block_rows, features), stored.dtype),
+            pltpu.VMEM((RING * ROW, block_rows, features), stored.dtype),
+            pltpu.VMEM((ROW,) + table.shape, jnp.int32),
+            pltpu.SMEM((ROW,) + table.shape, jnp.int32),
+            pltpu.SemaphoreType.DMA((8,)),
+            pltpu.SemaphoreType.DMA((8,)),
+            pltpu.SemaphoreType.DMA((ROW,)),
+            pltpu.SemaphoreType.DMA((ROW,)),
+            pltpu.SemaphoreType.DMA((RING, ROW)),
+            pltpu.SemaphoreType.DMA((RING, ROW)),
+            pltpu.SemaphoreType.DMA((2,)),
+        ],
+        compiler_params=pltpu.CompilerParams(
+            collective_id=0, has_side_effects=True, vmem_limit_bytes=48 * 1024 * 1024
+        ),
+        name="fetch",
+    )(slots, table, stored)
 
 
 def shards(query_emb, passage_emb, cand_blocks, positive):
-    dp_count = lax.axis_size("dp")
     fsdp_count = lax.axis_size("fsdp")
     query_blocks, list_len = cand_blocks.shape
     row_count, feature_count = query_emb.shape
     block_rows = row_count // query_blocks
     passage_blocks = passage_emb.shape[0] // block_rows
-    capacity = (list_len * query_blocks + dp_count - 1) // dp_count
-    slot_count = dp_count * capacity
     wanted = cand_blocks.reshape(-1)
     owners = wanted // passage_blocks
     local_ids = wanted % passage_blocks
-    placed = owners * capacity + slot_ranks(owners)
-    matched = lax.broadcasted_iota(jnp.int32, (slot_count, wanted.shape[0]), 0) == placed[None, :]
-    id_table = jnp.sum(jnp.where(matched, local_ids[None, :], 0), axis=1).reshape(
-        dp_count, capacity
-    )
-    requested = lax.all_to_all(id_table, "dp", split_axis=0, concat_axis=0, tiled=True)
+    owner_y = owners // ROW
+    owner_member = owners % ROW
+    at_member = owner_member[:, None, None] == lax.broadcasted_iota(jnp.int32, (1, ROW, 128), 1)
+    at_row = owner_y[:, None, None] == lax.broadcasted_iota(jnp.int32, (1, ROW, 128), 2)
+    table = jnp.sum(jnp.where(at_member & at_row, local_ids[:, None, None], 0), axis=0)
+    my_y = lax.axis_index("dp") // ROW
+    slots = ((my_y - owner_y + RING) % RING) * ROW + owner_member
     stored = passage_emb.reshape(passage_blocks, block_rows, feature_count)
-    outgoing = stored[requested]
-    fetched = lax.all_to_all(outgoing, "dp", split_axis=0, concat_axis=0, tiled=True)
-    candidates = fetched.reshape(slot_count, block_rows, feature_count)[placed]
+    candidates = fetch(slots, table, stored)
     candidates = candidates.reshape(query_blocks, list_len * block_rows, feature_count)
     query_rows = query_emb.reshape(query_blocks, block_rows, feature_count)
     partial_value = jnp.einsum(

time: 330 us -> 222 us (0.67)
  waiting for transfers between devices: 269 us -> 84.8 us
  Pallas kernels: 0 us -> 113 us
  blocking collectives: 18.3 us -> 0 us
  local copies, waits for them, and re-layouts: 11 us -> 2.63 us
  starting transfers between devices: 7.51 us -> 0.04 us
    all_to_all x1 -> x0, waiting for transfers between devices: 183 us -> none  [shards(): lax.all_to_all(outgoing, 'dp', split_axis=0, concat_axis=0, tiled=True)]
    pallas_call x0 -> x1, Pallas kernels: none -> 113 us  [fetch(): pl.pallas_call(fetch_kernel, out_shape=jax.ShapeDtypeStruct((slots.shape[...]
    all_to_all x1 -> x0, blocking collectives: 18.3 us -> none  [shards(): lax.all_to_all(id_table, 'dp', split_axis=0, concat_axis=0, tiled=True)]
    gather x2 -> x0, local copies, waits for them, and re-layouts: 9.39 us -> none  [the longest x1 5.33 us: shards(): outgoing = stored[requested]]
    all_to_all x1 -> x0, starting transfers between devices: 7.47 us -> none  [shards(): lax.all_to_all(outgoing, 'dp', split_axis=0, concat_axis=0, tiled=True)]
  transfers between devices with their start and end apart: 2 -> 1, of which waited for: 2 -> 1; matrix products, arithmetic and copies ran while one was open for 0% -> 0% of each run, Pallas kernels for 0% -> 0%
where the time goes in v1:
time: 222 us
  Pallas kernels  113 us (51%)
  waiting for transfers between devices  84.8 us (38%)
  between operations  14.1 us (6%)
  other arithmetic  3.74 us (2%)
  matrix products  3.09 us (1%)
  local copies, waits for them, and re-layouts  2.63 us (1%)
    pallas_call x1, Pallas kernels, fetch(): pl.pallas_call(fetch_kernel, out_shape=jax.ShapeDtypeStruct((slots.shape[...  113 us
    psum x1, waiting for transfers between devices, shards(): scores = lax.psum(partial_value, 'fsdp') * 50.0  84.8 us
  transfers between devices with their start and end apart: 1, of which 1 were waited for; matrix products, arithmetic and copies ran while one was open for 0% of the time, Pallas kernels for 0%

profile of v1, /device:TPU:6, one launch (start us, length us, event | category | flops | bytes accessed | tf_op | source)
XLA Modules:
  0.0 221.8 jit_solution(3559557856123891889)
XLA Ops:
  7.2 0.0 copy-start
  7.2 0.0 all-reduce.2.cloned.1.call-start
  7.2 0.8 reshape.117
  8.1 0.1 select_reduce_fusion.1.table_ref
  8.2 0.0 copy-start.1
  8.2 1.2 copy-done.1
  9.5 113.3 %fetch.1 = bf16[16,128,512]{2,1,0:T(8,128)(2,1)S(1)} custom-call(s32[16]{0:T(128)S(1)} %get-tuple-element.6.slots_ref, s32[8,128]{1,0:T(8,128)S(1)} %select_reduce_fusion.1.table_ref, bf16[8,128,512]{2,1,0:T(8,128)(2,1)S(1)} %bitcast.15), custom_call_target="tpu_custom_call" | custom-call | tf_op jit(solution)/shard_map/fetch/pallas_call | solution.py:147
  122.7 0.0 copy-done
  122.8 0.0 copy-start.3
  122.8 1.8 fusion.6
  124.6 0.0 all-reduce.2.cloned.1.call-update
  124.6 84.8 %all-reduce.2.cloned.1.call-done = f32[512,512]{1,0:T(8,128)} async-done(((f32[512,512]{1,0:T(8,128)}), f32[512,512]{1,0:T(8,128)}) %all-reduce.2.cloned.1.call-update) | async-done | bytes 1048592 | tf_op jit(solution)/shard_map/psum | solution.py:199
  209.5 0.0 copy-start.2
  209.5 1.5 multiply_reduce_fusion
  210.9 0.0 copy-done.3
  210.9 1.8 select_reduce_fusion
  212.7 0.0 copy-done.2
  212.8 0.3 subtract_convert_fusion
  213.1 1.2 fusion
  214.3 0.6 dynamic_slice.3
  (3 shorter events, 0.0 us)
Async XLA Ops:
  7.2 115.6 %copy-start = (bf16[512,512]{1,0:T(8,128)(2,1)S(1)}, bf16[512,512]{1,0:T(8,128)(2,1)}, u32[]{:S(2)}) copy-start(bf16[512,512]{1,0:T(8,128)(2,1)} %param.4) | copy-start | bytes 1572868
  7.2 202.3 %all-reduce.2.cloned.1.call-start = ((), (), s32[]{:S(2)}) async-start(), calls=%async_computation | async-start | bytes 2097152 | tf_op jit(solution)/shard_map/psum | solution.py:199
  8.2 1.2 copy-start.1
  122.8 88.2 %copy-start.3 = (s32[512]{0:T(512)S(1)}, s32[512]{0:T(512)}, u32[]{:S(2)}) copy-start(s32[512]{0:T(512)} %param.7) | copy-start | bytes 6148
  209.5 3.3 %copy-start.2 = (f32[512,512]{1,0:T(8,128)S(1)}, f32[512,512]{1,0:T(8,128)}, u32[]{:S(2)}) copy-start(f32[512,512]{1,0:T(8,128)} %all-reduce.2.cloned.1.call-done) | copy-start | bytes 3145732
Sparse Core Ops, SparseCore 0:
  124.8 84.6 all-reduce.1

commit v2 on v1

--- a/solution.py
+++ b/solution.py
@@ -8,29 +8,34 @@
 MESH = pl.DeviceIdType.MESH
 RING = 8
 ROW = 8
+Z = 8
 
 
 def softmax_rows(scores, positive_rows):
     row_max = jnp.max(scores, axis=1, keepdims=True)
-    log_total = row_max[:, 0] + jnp.log(jnp.sum(jnp.exp(scores - row_max), axis=1))
-    matched = lax.broadcasted_iota(jnp.int32, scores.shape, 1) == positive_rows[:, None]
-    losses = log_total - jnp.sum(jnp.where(matched, scores, jnp.float32(0.0)), axis=1)
-    weights = (jnp.exp(scores - log_total[:, None]) - matched.astype(jnp.float32)).astype(
-        jnp.bfloat16
+    log_total = row_max + jnp.log(jnp.sum(jnp.exp(scores - row_max), axis=1, keepdims=True))
+    matched = lax.broadcasted_iota(jnp.int32, scores.shape, 1) == positive_rows
+    losses = log_total - jnp.sum(
+        jnp.where(matched, scores, jnp.float32(0.0)), axis=1, keepdims=True
     )
+    weights = (jnp.exp(scores - log_total) - matched.astype(jnp.float32)).astype(jnp.bfloat16)
     return (losses, weights)
 
 
-def fetch_kernel(
-    slots_ref, table_ref, stored_ref, out_ref,
+def loss_kernel(
+    slots_ref, table_ref, positive_ref, query_ref, stored_ref, losses_ref, grad_ref,
     r1, r2, r3, l1, l2, l3, far, stage, got, tables, table_smem,
+    cands, sums_out, sums_in, weight_own, weight_in, weight_far,
     ring_send, ring_recv, table_send, table_recv, slot_send, slot_recv, local_sem,
+    sum_send, sum_recv, weight_send, weight_recv,
 ):
     me_dp = lax.axis_index("dp")
     y = me_dp // ROW
     member = me_dp % ROW
     up = ((y + 1) % RING) * ROW + member
     down = ((y + RING - 1) % RING) * ROW + member
+    z = lax.axis_index("fsdp")
+    z_targets = ((z + 1) % Z, (z + Z - 1) % Z)
 
     def peer_of(k):
         return (member + k) % ROW
@@ -41,13 +46,15 @@
     barrier = pltpu.get_barrier_semaphore()
     for target in (up, down):
         pl.semaphore_signal(barrier, inc=1, device_id={"dp": target}, device_id_type=MESH)
+    for target in z_targets:
+        pl.semaphore_signal(barrier, inc=1, device_id={"fsdp": target}, device_id_type=MESH)
 
     def greet(k, carry):
         pl.semaphore_signal(barrier, inc=1, device_id={"dp": row_dp(k)}, device_id_type=MESH)
         return carry
 
     lax.fori_loop(1, ROW, greet, 0)
-    pl.semaphore_wait(barrier, ROW + 1)
+    pl.semaphore_wait(barrier, ROW + 3)
 
     def ring_copy(index, src, dst, target):
         return pltpu.make_async_remote_copy(
@@ -134,47 +141,159 @@
         copy.wait_send()
 
     def place(i, carry):
-        out_ref[i] = got[slots_ref[i]]
-        return carry
-
-    lax.fori_loop(0, out_ref.shape[0], place, 0)
-
-
-def fetch(slots, table, stored):
+        cands[i] = got[slots_ref[i]]
+        return carry
+
+    lax.fori_loop(0, cands.shape[0], place, 0)
+
+    share, width = weight_own.shape
+    features = query_ref.shape[1]
+    list_len = width // cands.shape[1]
+    half_width, half_share = width // 2, share // 2
+
+    def listed(v):
+        return cands[pl.ds((v // 2) * list_len, list_len)].reshape(width, features)
+
+    def rows_of(v):
+        return pl.ds(pl.multiple_of(v * share, share), share)
+
+    def partial(offset):
+        v = (z + offset) % Z
+        value = lax.dot_general(
+            query_ref[rows_of(v), :], listed(v), (((1,), (1,)), ((), ())),
+            preferred_element_type=jnp.float32,
+        )
+        return (value[:, :half_width], value[:, half_width:])
+
+    def sum_copy(way, dist, c):
+        index = (way, dist - 1, c)
+        return pltpu.make_async_remote_copy(
+            src_ref=sums_out.at[index], dst_ref=sums_in.at[index],
+            send_sem=sum_send.at[index], recv_sem=sum_recv.at[index],
+            device_id={"fsdp": z_targets[way]}, device_id_type=MESH,
+        )
+
+    copies = []
+
+    def send_sum(way, dist, c, value):
+        sums_out[way, dist - 1, c] = value
+        copy = sum_copy(way, dist, c)
+        copy.start()
+        copies.append(copy)
+
+    farthest = partial(4)
+    send_sum(0, 4, 0, farthest[0])
+    send_sum(1, 4, 1, farthest[1])
+    for dist in (3, 2, 1):
+        values = (partial(dist), partial(Z - dist))
+        order = [(0, 0), (1, 1), (1, 0), (0, 1)]
+        if dist == 3:
+            order = order[2:] + order[:2]
+        for way, c in order:
+            value = values[way][c]
+            if dist < 3 or way == c:
+                sum_copy(way, dist + 1, c).wait_recv()
+                value = value + sums_in[way, dist, c]
+            send_sum(way, dist, c, value)
+    halves = list(partial(0))
+    for way, c in ((0, 0), (1, 1), (1, 0), (0, 1)):
+        sum_copy(way, 1, c).wait_recv()
+        halves[c] = halves[c] + sums_in[way, 0, c]
+    scores = jnp.concatenate(halves, axis=1) * 50.0
+    losses, weights = softmax_rows(scores, positive_ref[...])
+    weight_own[...] = weights
+    losses_ref[...] = losses
+
+    def part(ref, c):
+        return ref.at[pl.ds(c * half_share, half_share)]
+
+    def weight_copy(way, step, c):
+        source = weight_own if step == 0 else weight_in.at[way, step - 1]
+        target = weight_far if step == 3 else weight_in.at[way, step]
+        return pltpu.make_async_remote_copy(
+            src_ref=part(source, c), dst_ref=part(target, c),
+            send_sem=weight_send.at[way, step, c], recv_sem=weight_recv.at[way, step, c],
+            device_id={"fsdp": z_targets[way]}, device_id_type=MESH,
+        )
+
+    def send_weights(way, step, c):
+        copy = weight_copy(way, step, c)
+        copy.start()
+        copies.append(copy)
+
+    def gradient(rows, offset):
+        v = (z + offset) % Z
+        value = jnp.dot(rows, listed(v), preferred_element_type=jnp.float32) * 50.0
+        grad_ref[rows_of(v), :] = value.astype(grad_ref.dtype)
+
+    for c in range(2):
+        for way in range(2):
+            send_weights(way, 0, c)
+    gradient(weights, 0)
+    for step in range(1, 4):
+        for c in range(2):
+            for way in range(2):
+                weight_copy(way, step - 1, c).wait_recv()
+                if step < 3 or way == c:
+                    send_weights(way, step, c)
+        gradient(weight_in[0, step - 1], Z - step)
+        gradient(weight_in[1, step - 1], step)
+    for way in range(2):
+        weight_copy(way, 3, way).wait_recv()
+    gradient(weight_far[...], 4)
+    for copy in copies:
+        copy.wait_send()
+
+
+def loss_and_gradient(slots, table, positive_rows, query, stored):
     block_rows, features = stored.shape[1:]
-    shard = pltpu.VMEM(stored.shape, stored.dtype)
+    share = positive_rows.shape[0]
+    width = slots.shape[0] * block_rows * block_rows // query.shape[0]
     vmem = pl.BlockSpec(memory_space=pltpu.VMEM)
+    sums = pltpu.VMEM((2, 4, 2, share, width // 2), jnp.float32)
+    dma = pltpu.SemaphoreType.DMA
     return pl.pallas_call(
-        fetch_kernel,
-        out_shape=jax.ShapeDtypeStruct((slots.shape[0], block_rows, features), stored.dtype),
-        in_specs=[pl.BlockSpec(memory_space=pltpu.SMEM), vmem, vmem],
-        out_specs=vmem,
-        scratch_shapes=[shard] * 7
+        loss_kernel,
+        out_shape=(
+            jax.ShapeDtypeStruct((share, 1), jnp.float32),
+            jax.ShapeDtypeStruct(query.shape, query.dtype),
+        ),
+        in_specs=[pl.BlockSpec(memory_space=pltpu.SMEM), vmem, vmem, vmem, vmem],
+        out_specs=(vmem, vmem),
+        scratch_shapes=[pltpu.VMEM(stored.shape, stored.dtype)] * 7
         + [
             pltpu.VMEM((RING, ROW, block_rows, features), stored.dtype),
             pltpu.VMEM((RING * ROW, block_rows, features), stored.dtype),
             pltpu.VMEM((ROW,) + table.shape, jnp.int32),
             pltpu.SMEM((ROW,) + table.shape, jnp.int32),
-            pltpu.SemaphoreType.DMA((8,)),
-            pltpu.SemaphoreType.DMA((8,)),
-            pltpu.SemaphoreType.DMA((ROW,)),
-            pltpu.SemaphoreType.DMA((ROW,)),
-            pltpu.SemaphoreType.DMA((RING, ROW)),
-            pltpu.SemaphoreType.DMA((RING, ROW)),
-            pltpu.SemaphoreType.DMA((2,)),
+            pltpu.VMEM((slots.shape[0], block_rows, features), stored.dtype),
+            sums,
+            sums,
+            pltpu.VMEM((share, width), jnp.bfloat16),
+            pltpu.VMEM((2, 3, share, width), jnp.bfloat16),
+            pltpu.VMEM((share, width), jnp.bfloat16),
+            dma((8,)),
+            dma((8,)),
+            dma((ROW,)),
+            dma((ROW,)),
+            dma((RING, ROW)),
+            dma((RING, ROW)),
+            dma((2,)),
+            dma((2, 4, 2)),
+            dma((2, 4, 2)),
+            dma((2, 4, 2)),
+            dma((2, 4, 2)),
         ],
         compiler_params=pltpu.CompilerParams(
             collective_id=0, has_side_effects=True, vmem_limit_bytes=48 * 1024 * 1024
         ),
-        name="fetch",
-    )(slots, table, stored)
+        name="loss",
+    )(slots, table, positive_rows, query, stored)
 
 
 def shards(query_emb, passage_emb, cand_blocks, positive):
-    fsdp_count = lax.axis_size("fsdp")
-    query_blocks, list_len = cand_blocks.shape
     row_count, feature_count = query_emb.shape
-    block_rows = row_count // query_blocks
+    block_rows = row_count // cand_blocks.shape[0]
     passage_blocks = passage_emb.shape[0] // block_rows
     wanted = cand_blocks.reshape(-1)
     owners = wanted // passage_blocks
@@ -186,24 +305,12 @@
     table = jnp.sum(jnp.where(at_member & at_row, local_ids[:, None, None], 0), axis=0)
     my_y = lax.axis_index("dp") // ROW
     slots = ((my_y - owner_y + RING) % RING) * ROW + owner_member
+    share = row_count // Z
+    first_row = lax.axis_index("fsdp") * share
+    positive_rows = lax.dynamic_slice_in_dim(positive, first_row, share)[:, None]
     stored = passage_emb.reshape(passage_blocks, block_rows, feature_count)
-    candidates = fetch(slots, table, stored)
-    candidates = candidates.reshape(query_blocks, list_len * block_rows, feature_count)
-    query_rows = query_emb.reshape(query_blocks, block_rows, feature_count)
-    partial_value = jnp.einsum(
-        "qnd,qcd->qnc", query_rows, candidates, preferred_element_type=jnp.float32
-    )
-    partial_value = partial_value.reshape(row_count, list_len * block_rows)
-    share_rows = row_count // fsdp_count
-    first_row = lax.axis_index("fsdp") * share_rows
-    scores = lax.psum(partial_value, "fsdp") * 50.0
-    all_losses, weights = softmax_rows(scores, positive)
-    losses = lax.dynamic_slice_in_dim(all_losses, first_row, share_rows)
-    weights = weights.reshape(query_blocks, block_rows, list_len * block_rows)
-    query_grad = (
-        jnp.einsum("qnc,qcd->qnd", weights, candidates, preferred_element_type=jnp.float32) * 50.0
-    )
-    return (losses, query_grad.astype(jnp.bfloat16).reshape(row_count, feature_count))
+    losses, query_grad = loss_and_gradient(slots, table, positive_rows, query_emb, stored)
+    return (losses[:, 0], query_grad)
 
 
 def solution(mesh):

time: 222 us -> 158 us (0.71)
  waiting for transfers between devices: 84.8 us -> 0 us
  Pallas kernels: 113 us -> 151 us
  between operations: 14.1 us -> 0.68 us
  matrix products: 3.09 us -> 0 us
  other arithmetic: 3.74 us -> 0.78 us
    psum x1 -> x0, waiting for transfers between devices: 84.8 us -> none  [shards(): scores = lax.psum(partial_value, 'fsdp') * 50.0]
    pallas_call x1, Pallas kernels: 113 us -> 151 us  [loss_and_gradient(): pl.pallas_call(loss_kernel, out_shape=(jax.ShapeDtypeStruct((share, 1), j...]
    unnamed x8 -> x9, local copies, waits for them, and re-layouts: 1.24 us -> 4.33 us
    dot_general x2 -> x0, matrix products: 3.09 us -> none  [the longest x1 1.85 us: shards(): jnp.einsum('qnd,qcd->qnc', query_rows, candidates, preferred_element_type...]
  transfers between devices with their start and end apart: 1 -> 0, of which waited for: 1 -> 0; matrix products, arithmetic and copies ran while one was open for 0% -> 0% of each run, Pallas kernels for 0% -> 0%
where the time goes in v2:
time: 158 us; the launch traced here: 157 us
  Pallas kernels  151 us (96%)
  local copies, waits for them, and re-layouts  4.58 us (3%)
    pallas_call x1, Pallas kernels, loss_and_gradient(): pl.pallas_call(loss_kernel, out_shape=(jax.ShapeDtypeStruct((share, 1), j...  151 us
    unnamed x9, local copies, waits for them, and re-layouts  4.33 us

profile of v2, /device:TPU:6, one launch (start us, length us, event | category | flops | bytes accessed | tf_op | source)
XLA Modules:
  0.0 156.7 jit_solution(142631337484041701)
XLA Ops:
  0.6 0.0 copy-start
  0.7 0.7 copy-done
  1.3 0.0 copy-start.3
  1.3 0.1 dynamic-slice_bitcast_fusion
  1.4 0.6 copy-done.3
  2.0 0.1 reshape.94
  2.1 0.1 select_reduce_fusion.table_ref
  2.2 0.1 copy.8.positive_ref
  2.3 0.0 copy-start.1
  2.3 1.2 copy-done.1
  3.6 0.0 copy-start.2
  3.6 1.0 copy-done.2
  4.6 150.7 %loss.1 = (f32[64,1]{1,0:T(8,128)S(1)}, bf16[512,512]{1,0:T(8,128)(2,1)S(1)}) custom-call(s32[16]{0:T(128)S(1)} %get-tuple-element.6.slots_ref, s32[8,128]{1,0:T(8,128)S(1)} %select_reduce_fusion.table_ref, s32[64,1]{1,0:T(8,128)S(1)} %copy.8.positive_ref, bf16[512,512]{1,0:T(8,128)(2,1)S(1)} %copy-done.2, bf16[8,128,512]{2,1,0:T(8,128)(2,1)S(1)} %bitcast.3), custom_call_target="tpu_custom_call" | custom-call | tf_op jit(solution)/shard_map/loss/pallas_call | solution.py:255
  155.3 0.6 reduce
  156.0 0.8 copy.10
  (2 shorter events, 0.0 us)
Async XLA Ops:
  0.6 0.7 copy-start
  1.3 0.7 copy-start.3
  2.3 1.2 copy-start.1
  3.6 1.0 copy-start.2

commit v3 on v2

--- a/solution.py
+++ b/solution.py
@@ -9,6 +9,7 @@
 RING = 8
 ROW = 8
 Z = 8
+CHUNKS = 2
 
 
 def softmax_rows(scores, positive_rows):
@@ -23,12 +24,19 @@
 
 
 def loss_kernel(
-    slots_ref, table_ref, positive_ref, query_ref, stored_ref, losses_ref, grad_ref,
-    r1, r2, r3, l1, l2, l3, far, stage, got, tables, table_smem,
-    cands, sums_out, sums_in, weight_own, weight_in, weight_far,
-    ring_send, ring_recv, table_send, table_recv, slot_send, slot_recv, local_sem,
-    sum_send, sum_recv, weight_send, weight_recv,
+    slots_ref, table_ref, positive_ref, query_hbm, stored_hbm, losses_ref, grad_ref,
+    *scratch,
 ):
+    travelling = scratch[: 7 * CHUNKS]
+    (
+        query_ref, stored_ref, stage, got, tables, table_smem,
+        cands, sums_out, sums_in, weight_own, weight_in, weight_far,
+        ring_send, ring_recv, table_send, table_recv, slot_send, slot_recv, local_sem,
+        sum_send, sum_recv, weight_send, weight_recv,
+    ) = scratch[7 * CHUNKS :]
+    load_query = pltpu.make_async_copy(query_hbm, query_ref, local_sem.at[2])
+    load_stored = pltpu.make_async_copy(stored_hbm, stored_ref, local_sem.at[3])
+    load_stored.start()
     me_dp = lax.axis_index("dp")
     y = me_dp // ROW
     member = me_dp % ROW
@@ -56,23 +64,34 @@
     lax.fori_loop(1, ROW, greet, 0)
     pl.semaphore_wait(barrier, ROW + 3)
 
-    def ring_copy(index, src, dst, target):
-        return pltpu.make_async_remote_copy(
-            src_ref=src, dst_ref=dst, send_sem=ring_send.at[index], recv_sem=ring_recv.at[index],
-            device_id={"dp": target}, device_id_type=MESH,
-        )
-
-    half = stored_ref.shape[0] // 2
-    rights = [stored_ref, r1, r2, r3]
-    lefts = [stored_ref, l1, l2, l3]
-    right_copies = [ring_copy(d, rights[d], rights[d + 1], up) for d in range(3)]
-    left_copies = [ring_copy(4 + d, lefts[d], lefts[d + 1], down) for d in range(3)]
-    first, second = pl.ds(0, half), pl.ds(half, half)
-    right_copies.append(ring_copy(3, r3.at[first], far.at[first], up))
-    left_copies.append(ring_copy(7, l3.at[second], far.at[second], down))
-
-    right_copies[0].start()
-    left_copies[0].start()
+    chunk = stored_ref.shape[1] // CHUNKS
+
+    def arrived(way, c, d):
+        if d == 0:
+            return stored_hbm.at[:, pl.ds(c * chunk, chunk)]
+        return travelling[6 * CHUNKS + c if d == 4 else (3 * way + d - 1) * CHUNKS + c]
+
+    def ring_copy(way, c, d):
+        return pltpu.make_async_remote_copy(
+            src_ref=arrived(way, c, d), dst_ref=arrived(way, c, d + 1),
+            send_sem=ring_send.at[way, c, d], recv_sem=ring_recv.at[way, c, d],
+            device_id={"dp": (up, down)[way]}, device_id_type=MESH,
+        )
+
+    def passes(way, c, d):
+        return d < 3 or (d == 3 and c % 2 == way)
+
+    ring_copies = []
+
+    def pass_on(way, c, d):
+        if passes(way, c, d):
+            ring_copies.append(ring_copy(way, c, d))
+            ring_copies[-1].start()
+
+    for c in range(CHUNKS):
+        for way in range(2):
+            pass_on(way, c, 0)
+    load_query.start()
 
     def table_copy(k):
         return pltpu.make_async_remote_copy(
@@ -92,53 +111,58 @@
     lax.fori_loop(1, ROW, start_table, 0)
     own_table = pltpu.make_async_copy(table_ref, tables.at[member], local_sem.at[0])
     own_table.start()
+    lax.fori_loop(1, ROW, wait_table, 0)
     own_table.wait()
-    lax.fori_loop(1, ROW, wait_table, 0)
     to_smem = pltpu.make_async_copy(tables, table_smem, local_sem.at[1])
     to_smem.start()
     to_smem.wait()
 
-    def slot_copy(delta, k):
-        return pltpu.make_async_remote_copy(
-            src_ref=stage.at[delta, k], dst_ref=got.at[delta * ROW + member],
-            send_sem=slot_send.at[delta, k], recv_sem=slot_recv.at[delta, k],
+    def slot_copy(delta, c, k):
+        rows = pl.ds(c * chunk, chunk)
+        return pltpu.make_async_remote_copy(
+            src_ref=stage.at[delta, k, rows], dst_ref=got.at[delta * ROW + member, rows],
+            send_sem=slot_send.at[delta, c, k], recv_sem=slot_recv.at[delta, c, k],
             device_id={"dp": row_dp(k)}, device_id_type=MESH,
         )
 
-    def serve(delta, source):
+    def serve(delta, c, picked_from):
         owner_y = (y + RING - delta) % RING
+        rows = pl.ds(c * chunk, chunk)
 
         def picked(k):
-            chosen = table_smem[peer_of(k), member, owner_y]
-            return source[chosen]
+            return picked_from(table_smem[peer_of(k), member, owner_y])
 
         def send_one(k, carry):
-            stage[delta, k] = picked(k)
-            slot_copy(delta, k).start()
+            stage[delta, k, rows] = picked(k)
+            slot_copy(delta, c, k).start()
             return carry
 
         lax.fori_loop(1, ROW, send_one, 0)
-        got[delta * ROW + member] = picked(0)
-
-    serve(0, stored_ref)
-    for d in range(1, 4):
-        right_copies[d - 1].wait_recv()
-        right_copies[d].start()
-        left_copies[d - 1].wait_recv()
-        left_copies[d].start()
-        serve(d, rights[d])
-        serve(RING - d, lefts[d])
-    right_copies[3].wait_recv()
-    left_copies[3].wait_recv()
-    serve(4, far)
-
-    def wait_slot(index, carry):
-        slot_copy(index // (ROW - 1), index % (ROW - 1) + 1).wait()
-        return carry
-
-    lax.fori_loop(0, RING * (ROW - 1), wait_slot, 0)
-    for copy in right_copies + left_copies:
+        got[delta * ROW + member, rows] = picked(0)
+
+    load_stored.wait()
+    for c in range(CHUNKS):
+        serve(0, c, lambda chosen: stored_ref[chosen, pl.ds(c * chunk, chunk)])
+    for d in range(1, 5):
+        for c in range(CHUNKS):
+            ways = [way for way in range(2) if passes(way, c, d - 1)]
+            for way in ways:
+                ring_copy(way, c, d - 1).wait_recv()
+                pass_on(way, c, d)
+            for way in ways:
+                source = arrived(way, c, d)
+                serve(RING - d if way else d, c, lambda chosen: source[chosen])
+
+    for c in range(CHUNKS):
+
+        def wait_slot(index, carry):
+            slot_copy(index // (ROW - 1), c, index % (ROW - 1) + 1).wait()
+            return carry
+
+        lax.fori_loop(0, RING * (ROW - 1), wait_slot, 0)
+    for copy in ring_copies:
         copy.wait_send()
+    load_query.wait()
 
     def place(i, carry):
         cands[i] = got[slots_ref[i]]
@@ -250,6 +274,10 @@
     share = positive_rows.shape[0]
     width = slots.shape[0] * block_rows * block_rows // query.shape[0]
     vmem = pl.BlockSpec(memory_space=pltpu.VMEM)
+    hbm = pl.BlockSpec(memory_space=pltpu.HBM)
+    travelling = pltpu.VMEM(
+        (stored.shape[0], block_rows // CHUNKS, features), stored.dtype
+    )
     sums = pltpu.VMEM((2, 4, 2, share, width // 2), jnp.float32)
     dma = pltpu.SemaphoreType.DMA
     return pl.pallas_call(
@@ -258,10 +286,12 @@
             jax.ShapeDtypeStruct((share, 1), jnp.float32),
             jax.ShapeDtypeStruct(query.shape, query.dtype),
         ),
-        in_specs=[pl.BlockSpec(memory_space=pltpu.SMEM), vmem, vmem, vmem, vmem],
+        in_specs=[pl.BlockSpec(memory_space=pltpu.SMEM), vmem, vmem, hbm, hbm],
         out_specs=(vmem, vmem),
-        scratch_shapes=[pltpu.VMEM(stored.shape, stored.dtype)] * 7
+        scratch_shapes=[travelling] * (7 * CHUNKS)
         + [
+            pltpu.VMEM(query.shape, query.dtype),
+            pltpu.VMEM(stored.shape, stored.dtype),
             pltpu.VMEM((RING, ROW, block_rows, features), stored.dtype),
             pltpu.VMEM((RING * ROW, block_rows, features), stored.dtype),
             pltpu.VMEM((ROW,) + table.shape, jnp.int32),
@@ -272,13 +302,13 @@
             pltpu.VMEM((share, width), jnp.bfloat16),
             pltpu.VMEM((2, 3, share, width), jnp.bfloat16),
             pltpu.VMEM((share, width), jnp.bfloat16),
-            dma((8,)),
-            dma((8,)),
+            dma((2, CHUNKS, 4)),
+            dma((2, CHUNKS, 4)),
             dma((ROW,)),
             dma((ROW,)),
-            dma((RING, ROW)),
-            dma((RING, ROW)),
-            dma((2,)),
+            dma((RING, CHUNKS, ROW)),
+            dma((RING, CHUNKS, ROW)),
+            dma((4,)),
             dma((2, 4, 2)),
             dma((2, 4, 2)),
             dma((2, 4, 2)),

time: 158 us -> 150 us (0.949)
  Pallas kernels: 151 us -> 142 us
    pallas_call x1, Pallas kernels: 151 us -> 142 us  [loss_and_gradient(): pl.pallas_call(loss_kernel, out_shape=(jax.ShapeDtypeStruct((share, 1), j...]
where the time goes in v3:
time: 150 us; the launch traced here: 148 us
  Pallas kernels  142 us (95%)
  local copies, waits for them, and re-layouts  4.58 us (3%)
    pallas_call x1, Pallas kernels, loss_and_gradient(): pl.pallas_call(loss_kernel, out_shape=(jax.ShapeDtypeStruct((share, 1), j...  142 us
    unnamed x9, local copies, waits for them, and re-layouts  4.33 us

profile of v3, /device:TPU:6, one launch (start us, length us, event | category | flops | bytes accessed | tf_op | source)
XLA Modules:
  0.0 148.2 jit_solution(3409494735540616202)
XLA Ops:
  0.6 0.0 copy-start
  0.7 0.7 copy-done
  1.3 0.0 copy-start.3
  1.3 0.1 dynamic-slice_bitcast_fusion
  1.4 0.6 copy-done.3
  2.0 0.1 reshape.94
  2.1 0.1 select_reduce_fusion.table_ref
  2.2 0.1 copy.8.positive_ref
  2.3 0.0 copy-start.1
  2.3 1.2 copy-done.1
  3.6 0.0 copy-start.2
  3.6 1.0 copy-done.2
  4.6 142.2 %loss.1 = (f32[64,1]{1,0:T(8,128)S(1)}, bf16[512,512]{1,0:T(8,128)(2,1)S(1)}) custom-call(s32[16]{0:T(128)S(1)} %get-tuple-element.6.slots_ref, s32[8,128]{1,0:T(8,128)S(1)} %select_reduce_fusion.table_ref, s32[64,1]{1,0:T(8,128)S(1)} %copy.8.positive_ref, bf16[512,512]{1,0:T(8,128)(2,1)S(1)} %copy-done.2, bf16[8,128,512]{2,1,0:T(8,128)(2,1)S(1)} %bitcast.3), custom_call_target="tpu_custom_call" | custom-call | tf_op jit(solution)/shard_map/loss/pallas_call | solution.py:283
  146.8 0.6 reduce
  147.4 0.8 copy.10
  (2 shorter events, 0.0 us)
Async XLA Ops:
  0.6 0.7 copy-start
  1.3 0.7 copy-start.3
  2.3 1.2 copy-start.1
  3.6 1.0 copy-start.2

commit v4 on v3

v4 whole, which is shorter than its diff:
```python
import jax
import jax.numpy as jnp
from jax import lax
from jax.experimental import pallas as pl
from jax.experimental.pallas import tpu as pltpu
from jax.sharding import PartitionSpec as P

MESH = pl.DeviceIdType.MESH
RING = 8
ROW = 8
Z = 8
CHUNKS = 2
PIECES = 2


def softmax_rows(scores, matched):
    row_max = jnp.max(scores, axis=1, keepdims=True)
    log_total = row_max + jnp.log(jnp.sum(jnp.exp(scores - row_max), axis=1, keepdims=True))
    losses = log_total - jnp.sum(
        jnp.where(matched, scores, jnp.float32(0.0)), axis=1, keepdims=True
    )
    weights = (jnp.exp(scores - log_total) - matched.astype(jnp.float32)).astype(jnp.bfloat16)
    return (losses, weights)


def loss_kernel(
    slots_ref, table_ref, positive_ref, query_hbm, stored_hbm, losses_ref, grad_ref,
    *scratch,
):
    travelling = scratch[: 7 * CHUNKS]
    (
        query_ref, stored_ref, stage, got0, got1, tables, table_smem,
        cands0, cands1, sums_out, sums_in, weight_own, weight_in, weight_far,
        ring_send, ring_recv, table_send, table_recv, slot_send, slot_recv, local_sem,
        sum_send, sum_recv, weight_send, weight_recv,
    ) = scratch[7 * CHUNKS :]
    got, cands = (got0, got1), (cands0, cands1)
    load_query = pltpu.make_async_copy(query_hbm, query_ref, local_sem.at[2])
    load_stored = pltpu.make_async_copy(stored_hbm, stored_ref, local_sem.at[3])
    load_stored.start()
    me_dp = lax.axis_index("dp")
    y = me_dp // ROW
    member = me_dp % ROW
    up = ((y + 1) % RING) * ROW + member
    down = ((y + RING - 1) % RING) * ROW + member
    z = lax.axis_index("fsdp")
    z_targets = ((z + 1) % Z, (z + Z - 1) % Z)

    def peer_of(k):
        return (member + k) % ROW

    def row_dp(k):
        return y * ROW + peer_of(k)

    barrier = pltpu.get_barrier_semaphore()
    for target in (up, down):
        pl.semaphore_signal(barrier, inc=1, device_id={"dp": target}, device_id_type=MESH)
    for target in z_targets:
        pl.semaphore_signal(barrier, inc=1, device_id={"fsdp": target}, device_id_type=MESH)

    def greet(k, carry):
        pl.semaphore_signal(barrier, inc=1, device_id={"dp": row_dp(k)}, device_id_type=MESH)
        return carry

    lax.fori_loop(1, ROW, greet, 0)
    pl.semaphore_wait(barrier, ROW + 3)

    chunk = stored_ref.shape[1] // CHUNKS
    piece = chunk // PIECES

    def arrived(way, c, d):
        return travelling[6 * CHUNKS + c if d == 4 else (3 * way + d - 1) * CHUNKS + c]

    def piece_of(way, c, p, d):
        if d == 0:
            return stored_hbm.at[:, pl.ds(c * chunk + p * piece, piece)]
        return arrived(way, c, d).at[:, pl.ds(p * piece, piece)]

    def ring_copy(way, c, p, d):
        return pltpu.make_async_remote_copy(
            src_ref=piece_of(way, c, p, d), dst_ref=piece_of(way, c, p, d + 1),
            send_sem=ring_send.at[way, c, p, d], recv_sem=ring_recv.at[way, c, p, d],
            device_id={"dp": (up, down)[way]}, device_id_type=MESH,
        )

    def passes(way, p, d):
        return d < 3 or (d == 3 and p == way)

    ring_copies = []

    def pass_on(way, c, p, d):
        if passes(way, p, d):
            ring_copies.append(ring_copy(way, c, p, d))
            ring_copies[-1].start()

    def set_out(c):
        for p in range(PIECES):
            for way in range(2):
                pass_on(way, c, p, 0)

    def table_copy(k):
        return pltpu.make_async_remote_copy(
            src_ref=table_ref, dst_ref=tables.at[member],
            send_sem=table_send.at[k], recv_sem=table_recv.at[k],
            device_id={"dp": row_dp(k)}, device_id_type=MESH,
        )

    def start_table(k, carry):
        table_copy(k).start()
        return carry

    lax.fori_loop(1, ROW, start_table, 0)
    own_table = pltpu.make_async_copy(table_ref, tables.at[member], local_sem.at[0])
    own_table.start()
    set_out(0)
    load_query.start()

    def wait_table(k, carry):
        table_copy(k).wait()
        return carry

    lax.fori_loop(1, ROW, wait_table, 0)
    own_table.wait()
    to_smem = pltpu.make_async_copy(tables, table_smem, local_sem.at[1])
    to_smem.start()
    to_smem.wait()

    def slot_copy(delta, c, k):
        return pltpu.make_async_remote_copy(
            src_ref=stage.at[delta, k, pl.ds(c * chunk, chunk)],
            dst_ref=got[c].at[delta * ROW + member],
            send_sem=slot_send.at[delta, c, k], recv_sem=slot_recv.at[delta, c, k],
            device_id={"dp": row_dp(k)}, device_id_type=MESH,
        )

    def serve(delta, c, picked_from):
        owner_y = (y + RING - delta) % RING

        def picked(k):
            return picked_from(table_smem[peer_of(k), member, owner_y])

        def send_one(k, carry):
            stage[delta, k, pl.ds(c * chunk, chunk)] = picked(k)
            slot_copy(delta, c, k).start()
            return carry

        lax.fori_loop(1, ROW, send_one, 0)
        got[c][delta * ROW + member] = picked(0)

    share, width = weight_own.shape
    features = query_ref.shape[1]
    list_len = width // (CHUNKS * chunk)
    part_width = width // CHUNKS
    half_width, half_share = part_width // 2, share // 2
    copies = []

    def collect(c):
        def wait_slot(index, carry):
            slot_copy(index // (ROW - 1), c, index % (ROW - 1) + 1).wait()
            return carry

        def place(i, carry):
            cands[c][i] = got[c][slots_ref[i]]
            return carry

        lax.fori_loop(0, RING * (ROW - 1), wait_slot, 0)
        lax.fori_loop(0, cands[c].shape[0], place, 0)

    def listed(v, c):
        return cands[c][pl.ds((v // 2) * list_len, list_len)].reshape(part_width, features)

    def rows_of(v):
        return pl.ds(pl.multiple_of(v * share, share), share)

    def partial(c, offset):
        v = (z + offset) % Z
        value = lax.dot_general(
            query_ref[rows_of(v), :], listed(v, c), (((1,), (1,)), ((), ())),
            preferred_element_type=jnp.float32,
        )
        return (value[:, :half_width], value[:, half_width:])

    def sum_copy(c, way, dist, half):
        index = (c, way, dist - 1, half)
        return pltpu.make_async_remote_copy(
            src_ref=sums_out.at[index], dst_ref=sums_in.at[index],
            send_sem=sum_send.at[index], recv_sem=sum_recv.at[index],
            device_id={"fsdp": z_targets[way]}, device_id_type=MESH,
        )

    def send_sum(c, way, dist, half, value):
        sums_out[c, way, dist - 1, half] = value
        copies.append(sum_copy(c, way, dist, half))
        copies[-1].start()

    order = [(0, 0), (1, 1), (1, 0), (0, 1)]

    def sum_step(c, dist):
        values = (partial(c, dist), partial(c, Z - dist) if dist < 4 else None)
        if dist == 4:
            send_sum(c, 0, 4, 0, values[0][0])
            send_sum(c, 1, 4, 1, values[0][1])
            return
        for way, half in order[2:] + order[:2] if dist == 3 else order:
            value = values[way][half]
            if dist < 3 or way == half:
                sum_copy(c, way, dist + 1, half).wait_recv()
                value = value + sums_in[c, way, dist, half]
            send_sum(c, way, dist, half, value)

    def sum_end(c):
        halves = list(partial(c, 0))
        for way, half in order:
            sum_copy(c, way, 1, half).wait_recv()
            halves[half] = halves[half] + sums_in[c, way, 0, half]
        return halves

    load_stored.wait()
    for c in range(CHUNKS):
        serve(0, c, lambda chosen: stored_ref[chosen, pl.ds(c * chunk, chunk)])
    for c in range(CHUNKS):
        for d in range(1, 5):
            for p in range(PIECES):
                for way in range(2):
                    if passes(way, p, d - 1):
                        ring_copy(way, c, p, d - 1).wait_recv()
                        pass_on(way, c, p, d)
            if c == 0 and d == 3:
                set_out(1)
            for way in range(2 if d < 4 else 1):
                source = arrived(way, c, d)
                serve(RING - d if way else d, c, lambda chosen: source[chosen])
            if c == 1 and d == 2:
                load_query.wait()
                collect(0)
                sum_step(0, 4)
            if c == 1 and d == 3:
                sum_step(0, 3)
    sum_step(0, 2)
    sum_step(0, 1)
    halves = sum_end(0)
    collect(1)
    for dist in (4, 3, 2, 1):
        sum_step(1, dist)
    scores = jnp.concatenate(halves + sum_end(1), axis=1) * 50.0
    column = lax.broadcasted_iota(jnp.int32, scores.shape, 1)
    position = (
        (column % part_width // chunk) * (CHUNKS * chunk)
        + (column // part_width) * chunk
        + column % chunk
    )
    losses, weights = softmax_rows(scores, position == positive_ref[...])
    weight_own[...] = weights
    losses_ref[...] = losses

    def part(ref, c):
        return ref.at[pl.ds(c * half_share, half_share)]

    def weight_copy(way, step, c):
        source = weight_own if step == 0 else weight_in.at[way, step - 1]
        target = weight_far if step == 3 else weight_in.at[way, step]
        return pltpu.make_async_remote_copy(
            src_ref=part(source, c), dst_ref=part(target, c),
            send_sem=weight_send.at[way, step, c], recv_sem=weight_recv.at[way, step, c],
            device_id={"fsdp": z_targets[way]}, device_id_type=MESH,
        )

    def send_weights(way, step, c):
        copy = weight_copy(way, step, c)
        copy.start()
        copies.append(copy)

    def gradient(rows, offset):
        v = (z + offset) % Z
        value = sum(
            jnp.dot(
                rows[:, c * part_width : (c + 1) * part_width], listed(v, c),
                preferred_element_type=jnp.float32,
            )
            for c in range(CHUNKS)
        )
        grad_ref[rows_of(v), :] = (value * 50.0).astype(grad_ref.dtype)

    for c in range(2):
        for way in range(2):
            send_weights(way, 0, c)
    gradient(weights, 0)
    for step in range(1, 4):
        for c in range(2):
            for way in range(2):
                weight_copy(way, step - 1, c).wait_recv()
                if step < 3 or way == c:
                    send_weights(way, step, c)
        gradient(weight_in[0, step - 1], Z - step)
        gradient(weight_in[1, step - 1], step)
    for way in range(2):
        weight_copy(way, 3, way).wait_recv()
    gradient(weight_far[...], 4)
    for copy in copies + ring_copies:
        copy.wait_send()


def loss_and_gradient(slots, table, positive_rows, query, stored):
    block_rows, features = stored.shape[1:]
    share = positive_rows.shape[0]
    width = slots.shape[0] * block_rows * block_rows // query.shape[0]
    vmem = pl.BlockSpec(memory_space=pltpu.VMEM)
    hbm = pl.BlockSpec(memory_space=pltpu.HBM)
    travelling = pltpu.VMEM(
        (stored.shape[0], block_rows // CHUNKS, features), stored.dtype
    )
    chunk = block_rows // CHUNKS
    sums = pltpu.VMEM((CHUNKS, 2, 4, 2, share, width // CHUNKS // 2), jnp.float32)
    dma = pltpu.SemaphoreType.DMA
    return pl.pallas_call(
        loss_kernel,
        out_shape=(
            jax.ShapeDtypeStruct((share, 1), jnp.float32),
            jax.ShapeDtypeStruct(query.shape, query.dtype),
        ),
        in_specs=[pl.BlockSpec(memory_space=pltpu.SMEM), vmem, vmem, hbm, hbm],
        out_specs=(vmem, vmem),
        scratch_shapes=[travelling] * (7 * CHUNKS)
        + [
            pltpu.VMEM(query.shape, query.dtype),
            pltpu.VMEM(stored.shape, stored.dtype),
            pltpu.VMEM((RING, ROW, block_rows, features), stored.dtype),
            pltpu.VMEM((RING * ROW, chunk, features), stored.dtype),
            pltpu.VMEM((RING * ROW, chunk, features), stored.dtype),
            pltpu.VMEM((ROW,) + table.shape, jnp.int32),
            pltpu.SMEM((ROW,) + table.shape, jnp.int32),
            pltpu.VMEM((slots.shape[0], chunk, features), stored.dtype),
            pltpu.VMEM((slots.shape[0], chunk, features), stored.dtype),
            sums,
            sums,
            pltpu.VMEM((share, width), jnp.bfloat16),
            pltpu.VMEM((2, 3, share, width), jnp.bfloat16),
            pltpu.VMEM((share, width), jnp.bfloat16),
            dma((2, CHUNKS, PIECES, 4)),
            dma((2, CHUNKS, PIECES, 4)),
            dma((ROW,)),
            dma((ROW,)),
            dma((RING, CHUNKS, ROW)),
            dma((RING, CHUNKS, ROW)),
            dma((4,)),
            dma((CHUNKS, 2, 4, 2)),
            dma((CHUNKS, 2, 4, 2)),
            dma((2, 4, 2)),
            dma((2, 4, 2)),
        ],
        compiler_params=pltpu.CompilerParams(
            collective_id=0, has_side_effects=True, vmem_limit_bytes=48 * 1024 * 1024
        ),
        name="loss",
    )(slots, table, positive_rows, query, stored)


def shards(query_emb, passage_emb, cand_blocks, positive):
    row_count, feature_count = query_emb.shape
    block_rows = row_count // cand_blocks.shape[0]
    passage_blocks = passage_emb.shape[0] // block_rows
    wanted = cand_blocks.reshape(-1)
    owners = wanted // passage_blocks
    local_ids = wanted % passage_blocks
    owner_y = owners // ROW
    owner_member = owners % ROW
    at_member = owner_member[:, None, None] == lax.broadcasted_iota(jnp.int32, (1, ROW, 128), 1)
    at_row = owner_y[:, None, None] == lax.broadcasted_iota(jnp.int32, (1, ROW, 128), 2)
    table = jnp.sum(jnp.where(at_member & at_row, local_ids[:, None, None], 0), axis=0)
    my_y = lax.axis_index("dp") // ROW
    slots = ((my_y - owner_y + RING) % RING) * ROW + owner_member
    share = row_count // Z
    first_row = lax.axis_index("fsdp") * share
    positive_rows = lax.dynamic_slice_in_dim(positive, first_row, share)[:, None]
    stored = passage_emb.reshape(passage_blocks, block_rows, feature_count)
    losses, query_grad = loss_and_gradient(slots, table, positive_rows, query_emb, stored)
    return (losses[:, 0], query_grad)


def solution(mesh):
    return jax.shard_map(
        shards,
        mesh=mesh,
        in_specs=(P("dp", "fsdp"), P("dp", "fsdp"), P("dp", None), P("dp")),
        out_specs=(P(("dp", "fsdp")), P("dp", "fsdp")),
        check_vma=False,
    )
```

time: 150 us -> 148 us (0.987)
  Pallas kernels: 142 us -> 140 us
    pallas_call x1, Pallas kernels: 142 us -> 140 us  [loss_and_gradient(): pl.pallas_call(loss_kernel, out_shape=(jax.ShapeDtypeStruct((share, 1), j...]
where the time goes in v4:
time: 148 us; the launch traced here: 146 us
  Pallas kernels  140 us (95%)
  local copies, waits for them, and re-layouts  4.58 us (3%)
    pallas_call x1, Pallas kernels, loss_and_gradient(): pl.pallas_call(loss_kernel, out_shape=(jax.ShapeDtypeStruct((share, 1), j...  140 us
    unnamed x9, local copies, waits for them, and re-layouts  4.33 us

profile of v4, /device:TPU:6, one launch (start us, length us, event | category | flops | bytes accessed | tf_op | source)
XLA Modules:
  0.0 146.2 jit_solution(18247720790374903337)
XLA Ops:
  0.6 0.0 copy-start
  0.7 0.7 copy-done
  1.3 0.0 copy-start.3
  1.3 0.1 dynamic-slice_bitcast_fusion
  1.4 0.6 copy-done.3
  2.0 0.1 reshape.94
  2.1 0.1 select_reduce_fusion.table_ref
  2.2 0.1 copy.8.positive_ref
  2.3 0.0 copy-start.1
  2.3 1.2 copy-done.1
  3.6 0.0 copy-start.2
  3.6 1.0 copy-done.2
  4.6 140.1 %loss.1 = (f32[64,1]{1,0:T(8,128)S(1)}, bf16[512,512]{1,0:T(8,128)(2,1)S(1)}) custom-call(s32[16]{0:T(128)S(1)} %get-tuple-element.6.slots_ref, s32[8,128]{1,0:T(8,128)S(1)} %select_reduce_fusion.table_ref, s32[64,1]{1,0:T(8,128)S(1)} %copy.8.positive_ref, bf16[512,512]{1,0:T(8,128)(2,1)S(1)} %copy-done.2, bf16[8,128,512]{2,1,0:T(8,128)(2,1)S(1)} %bitcast.3), custom_call_target="tpu_custom_call" | custom-call | tf_op jit(solution)/shard_map/loss/pallas_call | solution.py:315
  144.8 0.6 reduce
  145.4 0.8 copy.10
  (2 shorter events, 0.0 us)
Async XLA Ops:
  0.6 0.7 copy-start
  1.3 0.7 copy-start.3
  2.3 1.2 copy-start.1
  3.6 1.0 copy-start.2

commit v5 on v4

--- a/solution.py
+++ b/solution.py
@@ -125,27 +125,32 @@
     to_smem.start()
     to_smem.wait()
 
-    def slot_copy(delta, c, k):
+    def slot_copy(group, c, k, size):
+        first = (group - 1) * 2 * ROW + 2 * member if size == 2 else (6 + group // 4) * ROW + member
         return pltpu.make_async_remote_copy(
-            src_ref=stage.at[delta, k, pl.ds(c * chunk, chunk)],
-            dst_ref=got[c].at[delta * ROW + member],
-            send_sem=slot_send.at[delta, c, k], recv_sem=slot_recv.at[delta, c, k],
+            src_ref=stage.at[group, c, k, pl.ds(0, size)], dst_ref=got[c].at[pl.ds(first, size)],
+            send_sem=slot_send.at[group, c, k], recv_sem=slot_recv.at[group, c, k],
             device_id={"dp": row_dp(k)}, device_id_type=MESH,
         )
 
-    def serve(delta, c, picked_from):
-        owner_y = (y + RING - delta) % RING
-
-        def picked(k):
+    def serve(group, c, sources):
+        size = len(sources)
+
+        def picked(k, way):
+            delta, picked_from = sources[way]
+            owner_y = (y + RING - delta) % RING
             return picked_from(table_smem[peer_of(k), member, owner_y])
 
         def send_one(k, carry):
-            stage[delta, k, pl.ds(c * chunk, chunk)] = picked(k)
-            slot_copy(delta, c, k).start()
+            for way in range(size):
+                stage[group, c, k, way] = picked(k, way)
+            slot_copy(group, c, k, size).start()
             return carry
 
         lax.fori_loop(1, ROW, send_one, 0)
-        got[c][delta * ROW + member] = picked(0)
+        first = (group - 1) * 2 * ROW + 2 * member if size == 2 else (6 + group // 4) * ROW + member
+        for way in range(size):
+            got[c][first + way] = picked(0, way)
 
     share, width = weight_own.shape
     features = query_ref.shape[1]
@@ -155,15 +160,18 @@
     copies = []
 
     def collect(c):
-        def wait_slot(index, carry):
-            slot_copy(index // (ROW - 1), c, index % (ROW - 1) + 1).wait()
-            return carry
-
         def place(i, carry):
             cands[c][i] = got[c][slots_ref[i]]
             return carry
 
-        lax.fori_loop(0, RING * (ROW - 1), wait_slot, 0)
+        for group in range(5):
+
+            def wait_slot(k, carry):
+                slot_copy(group, c, k, 2 if group % 4 else 1).wait()
+                return carry
+
+            lax.fori_loop(1, ROW, wait_slot, 0)
+
         lax.fori_loop(0, cands[c].shape[0], place, 0)
 
     def listed(v, c):
@@ -217,7 +225,7 @@
 
     load_stored.wait()
     for c in range(CHUNKS):
-        serve(0, c, lambda chosen: stored_ref[chosen, pl.ds(c * chunk, chunk)])
+        serve(0, c, [(0, lambda chosen: stored_ref[chosen, pl.ds(c * chunk, chunk)])])
     for c in range(CHUNKS):
         for d in range(1, 5):
             for p in range(PIECES):
@@ -227,9 +235,14 @@
                         pass_on(way, c, p, d)
             if c == 0 and d == 3:
                 set_out(1)
-            for way in range(2 if d < 4 else 1):
-                source = arrived(way, c, d)
-                serve(RING - d if way else d, c, lambda chosen: source[chosen])
+            shards_in = [arrived(way, c, d) for way in range(2 if d < 4 else 1)]
+            serve(
+                d, c,
+                [
+                    (RING - d if way else d, lambda chosen, shard=shard: shard[chosen])
+                    for way, shard in enumerate(shards_in)
+                ],
+            )
             if c == 1 and d == 2:
                 load_query.wait()
                 collect(0)
@@ -324,7 +337,7 @@
         + [
             pltpu.VMEM(query.shape, query.dtype),
             pltpu.VMEM(stored.shape, stored.dtype),
-            pltpu.VMEM((RING, ROW, block_rows, features), stored.dtype),
+            pltpu.VMEM((5, CHUNKS, ROW, 2, chunk, features), stored.dtype),
             pltpu.VMEM((RING * ROW, chunk, features), stored.dtype),
             pltpu.VMEM((RING * ROW, chunk, features), stored.dtype),
             pltpu.VMEM((ROW,) + table.shape, jnp.int32),
@@ -340,8 +353,8 @@
             dma((2, CHUNKS, PIECES, 4)),
             dma((ROW,)),
             dma((ROW,)),
-            dma((RING, CHUNKS, ROW)),
-            dma((RING, CHUNKS, ROW)),
+            dma((5, CHUNKS, ROW)),
+            dma((5, CHUNKS, ROW)),
             dma((4,)),
             dma((CHUNKS, 2, 4, 2)),
             dma((CHUNKS, 2, 4, 2)),
@@ -368,7 +381,13 @@
     at_row = owner_y[:, None, None] == lax.broadcasted_iota(jnp.int32, (1, ROW, 128), 2)
     table = jnp.sum(jnp.where(at_member & at_row, local_ids[:, None, None], 0), axis=0)
     my_y = lax.axis_index("dp") // ROW
-    slots = ((my_y - owner_y + RING) % RING) * ROW + owner_member
+    delta = (my_y - owner_y + RING) % RING
+    pair = jnp.minimum(delta, RING - delta)
+    slots = jnp.where(
+        pair % 4 == 0,
+        (6 + pair // 4) * ROW + owner_member,
+        ((pair - 1) * ROW + owner_member) * 2 + (delta > 4),
+    )
     share = row_count // Z
     first_row = lax.axis_index("fsdp") * share
     positive_rows = lax.dynamic_slice_in_dim(positive, first_row, share)[:, None]

time: 148 us -> 146 us (0.986)
  no operation moved by 1% of the time
where the time goes in v5:
time: 146 us; the launch traced here: 145 us
  Pallas kernels  139 us (95%)
  local copies, waits for them, and re-layouts  4.58 us (3%)
    pallas_call x1, Pallas kernels, loss_and_gradient(): pl.pallas_call(loss_kernel, out_shape=(jax.ShapeDtypeStruct((share, 1), j...  139 us
    unnamed x9, local copies, waits for them, and re-layouts  4.33 us

profile of v5, /device:TPU:6, one launch (start us, length us, event | category | flops | bytes accessed | tf_op | source)
XLA Modules:
  0.0 145.0 jit_solution(15168330062512247769)
XLA Ops:
  0.6 0.0 copy-start
  0.7 0.7 copy-done
  1.3 0.0 copy-start.3
  1.3 0.1 dynamic-slice_bitcast_fusion
  1.4 0.6 copy-done.3
  2.0 0.1 reshape.94
  2.1 0.1 select_reduce_fusion.table_ref
  2.3 0.1 copy.8.positive_ref
  2.4 0.0 copy-start.1
  2.4 1.2 copy-done.1
  3.6 0.0 copy-start.2
  3.6 1.0 copy-done.2
  4.6 138.9 %loss.1 = (f32[64,1]{1,0:T(8,128)S(1)}, bf16[512,512]{1,0:T(8,128)(2,1)S(1)}) custom-call(s32[16]{0:T(128)S(1)} %get-tuple-element.6.slots_ref, s32[8,128]{1,0:T(8,128)S(1)} %select_reduce_fusion.table_ref, s32[64,1]{1,0:T(8,128)S(1)} %copy.8.positive_ref, bf16[512,512]{1,0:T(8,128)(2,1)S(1)} %copy-done.2, bf16[8,128,512]{2,1,0:T(8,128)(2,1)S(1)} %bitcast.3), custom_call_target="tpu_custom_call" | custom-call | tf_op jit(solution)/shard_map/loss/pallas_call | solution.py:328
  143.6 0.6 reduce
  144.2 0.8 copy.10
  (2 shorter events, 0.0 us)
Async XLA Ops:
  0.6 0.7 copy-start
  1.3 0.7 copy-start.3
  2.4 1.2 copy-start.1
  3.6 1.0 copy-start.2

commit v6 on v5

--- a/solution.py
+++ b/solution.py
@@ -264,7 +264,11 @@
     )
     losses, weights = softmax_rows(scores, position == positive_ref[...])
     weight_own[...] = weights
-    losses_ref[...] = losses
+    square = (share, share)
+    diagonal = lax.broadcasted_iota(jnp.int32, square, 0) == lax.broadcasted_iota(
+        jnp.int32, square, 1
+    )
+    losses_ref[...] = jnp.sum(jnp.where(diagonal, losses, 0.0), axis=0, keepdims=True)
 
     def part(ref, c):
         return ref.at[pl.ds(c * half_share, half_share)]
@@ -328,7 +332,7 @@
     return pl.pallas_call(
         loss_kernel,
         out_shape=(
-            jax.ShapeDtypeStruct((share, 1), jnp.float32),
+            jax.ShapeDtypeStruct((1, share), jnp.float32),
             jax.ShapeDtypeStruct(query.shape, query.dtype),
         ),
         in_specs=[pl.BlockSpec(memory_space=pltpu.SMEM), vmem, vmem, hbm, hbm],
@@ -393,7 +397,7 @@
     positive_rows = lax.dynamic_slice_in_dim(positive, first_row, share)[:, None]
     stored = passage_emb.reshape(passage_blocks, block_rows, feature_count)
     losses, query_grad = loss_and_gradient(slots, table, positive_rows, query_emb, stored)
-    return (losses[:, 0], query_grad)
+    return (losses[0], query_grad)
 
 
 def solution(mesh):

time: 146 us -> 146 us (level)
    unnamed x9 -> x10, local copies, waits for them, and re-layouts: 4.33 us -> 4.84 us
where the time goes in v6:
time: 146 us; the launch traced here: 145 us
  Pallas kernels  139 us (95%)
  local copies, waits for them, and re-layouts  5.09 us (3%)
    pallas_call x1, Pallas kernels, loss_and_gradient(): pl.pallas_call(loss_kernel, out_shape=(jax.ShapeDtypeStruct((1, share), j...  139 us
    unnamed x10, local copies, waits for them, and re-layouts  4.84 us

profile of v6, /device:TPU:6, one launch (start us, length us, event | category | flops | bytes accessed | tf_op | source)
XLA Modules:
  0.0 144.9 jit_solution(13852245762476807922)
XLA Ops:
  0.6 0.0 copy-start
  0.7 0.7 copy-done
  1.3 0.0 copy-start.3
  1.3 0.1 dynamic-slice_bitcast_fusion
  1.4 0.6 copy-done.3
  2.0 0.1 reshape.94
  2.1 0.1 select_reduce_fusion.table_ref
  2.3 0.1 copy.7.positive_ref
  2.4 0.0 copy-start.1
  2.4 1.2 copy-done.1
  3.6 0.0 copy-start.2
  3.6 1.0 copy-done.2
  4.6 138.9 %loss.1 = (f32[1,64]{1,0:T(1,128)S(1)}, bf16[512,512]{1,0:T(8,128)(2,1)S(1)}) custom-call(s32[16]{0:T(128)S(1)} %get-tuple-element.6.slots_ref, s32[8,128]{1,0:T(8,128)S(1)} %select_reduce_fusion.table_ref, s32[64,1]{1,0:T(8,128)S(1)} %copy.7.positive_ref, bf16[512,512]{1,0:T(8,128)(2,1)S(1)} %copy-done.2, bf16[8,128,512]{2,1,0:T(8,128)(2,1)S(1)} %bitcast.4), custom_call_target="tpu_custom_call" | custom-call | tf_op jit(solution)/shard_map/loss/pallas_call | solution.py:332
  143.6 0.5 copy.10
  144.1 0.8 copy.11
  (2 shorter events, 0.0 us)
Async XLA Ops:
  0.6 0.7 copy-start
  1.3 0.7 copy-start.3
  2.4 1.2 copy-start.1
  3.6 1.0 copy-start.2
